TPU v7x, 32 devices: a whole 2x2x4 slice. The times are simulated.
32 devices in a mesh: dp: 16 (over z, x, core), mp: 2 (over y).
Axes of the slice: x: 2, y: 2, z: 4, core: 2. Of those that a mesh axis runs over, the one named last changes fastest.
Arguments:
- tokens: bfloat16 [512, 16384], P('dp', 'mp'), may hold values from -6 to 6
- gate_weight: bfloat16 [16384, 28672], P('mp', 'dp'), may hold values from -0.046875 to 0.046875
- up_weight: bfloat16 [16384, 28672], P('mp', 'dp'), may hold values from -0.046875 to 0.046875
- down_weight: bfloat16 [28672, 16384], P('dp', 'mp'), may hold values from -0.03125 to 0.03125
Outputs:
- mixed: bfloat16 [512, 16384], P('dp', 'mp')
All inputs are finite; a program needn't handle non-finite values.
Results may differ from a plain program's by a relative error of at most 0.0049.
Values may be sent and summed in bfloat16 or wider, within the bound.
No kernel may reach another device: no remote copies, remote signals or barrier semaphores. Data moves between devices by JAX's collectives and lax.ppermute only.
A program may use at most 192 MiB of HBM per device.

v0:
```python
import jax
import jax.numpy as jnp
from jax import lax
from jax.sharding import PartitionSpec as P


def per_device(tokens, gate_weight, up_weight, down_weight):
    width = gate_weight.shape[1]
    piece = lax.all_gather(tokens, "dp", axis=0, tiled=True)
    gate_part = jnp.dot(piece, gate_weight, preferred_element_type=jnp.float32)
    up_part = jnp.dot(piece, up_weight, preferred_element_type=jnp.float32)
    partial_both = jnp.concatenate([gate_part, up_part], axis=1)
    share = lax.psum_scatter(partial_both, "mp", scatter_dimension=0, tiled=True)
    own_rows = (jax.nn.silu(share[:, :width]) * share[:, width:]).astype(jnp.bfloat16)
    hidden = lax.all_gather(own_rows, "mp", axis=0, tiled=True)
    mixed = lax.psum_scatter(
        jnp.dot(hidden, down_weight, preferred_element_type=jnp.float32),
        "dp",
        scatter_dimension=0,
        tiled=True,
    )
    return mixed.astype(jnp.bfloat16)


def solution(mesh):
    return jax.shard_map(
        per_device,
        mesh=mesh,
        in_specs=(P("dp", "mp"), P("mp", "dp"), P("mp", "dp"), P("dp", "mp")),
        out_specs=P("dp", "mp"),
        check_vma=False,
    )
```

profile of v0, /device:TPU:0, one launch (start us, length us, event | category | flops | bytes accessed | tf_op | source)
XLA Modules:
  0.0 462.6 jit_solution(2330269825002777299)
XLA Ops:
  6.5 0.0 all-gather.3.cloned.1.call-start
  6.5 0.7 all-gather.3.cloned.1.call-update
  7.3 0.0 reduce-scatter.3.cloned.1.call-start
  7.3 79.2 %all-gather.3.cloned.1.call-done = bf16[512,8192]{1,0:T(8,128)(2,1)} async-done(((bf16[32,8192]{1,0:T(8,128)(2,1)}), bf16[512,8192]{1,0:T(8,128)(2,1)}) %all-gather.3.cloned.1.call-update) | async-done | bytes 8388624 | tf_op jit(solution)/shard_map/all_gather | solution.py:9
  86.5 0.0 copy-start
  86.5 21.3 %fusion.2 = f32[512,1792]{1,0:T(8,128)S(1)} fusion(bf16[512,8192]{1,0:T(8,128)(2,1)} %all-gather.3.cloned.1.call-done, bf16[8192,1792]{1,0:T(8,128)(2,1)} %param.6), kind=kOutput, calls=%fused_computation.4 | convolution fusion | flops 15032385536 | bytes 41418752 | tf_op jit(solution)/shard_map/dot_general | solution.py:11
  107.8 0.0 copy-done
  107.8 19.2 %fusion.1 = f32[512,1792]{1,0:T(8,128)S(1)} fusion(bf16[512,8192]{1,0:T(8,128)(2,1)S(1)} %copy-done, bf16[8192,1792]{1,0:T(8,128)(2,1)} %param.5), kind=kOutput, calls=%fused_computation.3 | convolution fusion | flops 15032385536 | bytes 41418752 | tf_op jit(solution)/shard_map/dot_general | solution.py:10
  127.0 4.0 pad_maximum_fusion
  131.1 0.0 reduce-scatter.3.cloned.1.call-update
  131.1 0.0 all-gather.5.cloned.1.call-start
  131.1 87.2 %reduce-scatter.3.cloned.1.call-done = f32[256,3584]{1,0:T(8,128)} async-done(((f32[512,3584]{1,0:T(8,128)}), f32[256,3584]{1,0:T(8,128)}) %reduce-scatter.3.cloned.1.call-update) | async-done | bytes 3670032 | tf_op jit(solution)/shard_map/reduce_scatter | solution.py:13
  218.3 3.5 fusion
  221.8 0.0 all-gather.5.cloned.1.call-update
  221.8 0.2 reduce-scatter.5.cloned.1.call-start
  222.1 30.1 %all-gather.5.cloned.1.call-done = bf16[512,1792]{1,0:T(8,128)(2,1)} async-done(((bf16[256,1792]{1,0:T(8,128)(2,1)}), bf16[512,1792]{1,0:T(8,128)(2,1)}) %all-gather.5.cloned.1.call-update) | async-done | bytes 1835024 | tf_op jit(solution)/shard_map/all_gather | solution.py:15
  252.1 24.4 %fusion.3 = f32[512,8192]{1,0:T(8,128)} fusion(bf16[512,1792]{1,0:T(8,128)(2,1)} %all-gather.5.cloned.1.call-done, bf16[1792,8192]{1,0:T(8,128)(2,1)} %param.7), kind=kOutput, calls=%fused_computation.5 | convolution fusion | flops 15032385536 | bytes 47972352 | tf_op jit(solution)/shard_map/dot_general | solution.py:17
  276.5 0.0 reduce-scatter.5.cloned.1.call-update
  276.6 177.5 %reduce-scatter.5.cloned.1.call-done = f32[32,8192]{1,0:T(8,128)} async-done(((f32[512,8192]{1,0:T(8,128)}), f32[32,8192]{1,0:T(8,128)}) %reduce-scatter.5.cloned.1.call-update) | async-done | bytes 1048592 | tf_op jit(solution)/shard_map/reduce_scatter | solution.py:16
  454.0 2.1 convert_element_type.7
Async XLA Ops:
  6.5 80.0 %all-gather.3.cloned.1.call-start = ((), (), s32[]{:S(2)}) async-start(), calls=%async_computation.2 | async-start | bytes 8912896 | tf_op jit(solution)/shard_map/all_gather | solution.py:9
  7.3 211.1 %reduce-scatter.3.cloned.1.call-start = ((), (), s32[]{:S(2)}) async-start(), calls=%async_computation.3 | async-start | bytes 11010048 | tf_op jit(solution)/shard_map/reduce_scatter | solution.py:13
  86.5 21.3 %copy-start = (bf16[512,8192]{1,0:T(8,128)(2,1)S(1)}, bf16[512,8192]{1,0:T(8,128)(2,1)}, u32[]{:S(2)}) copy-start(bf16[512,8192]{1,0:T(8,128)(2,1)} %all-gather.3.cloned.1.call-done) | copy-start | bytes 25165828
  131.1 121.1 %all-gather.5.cloned.1.call-start = ((), (), s32[]{:S(2)}) async-start(), calls=%async_computation.4 | async-start | bytes 2752512 | tf_op jit(solution)/shard_map/all_gather | solution.py:15
  221.8 232.2 %reduce-scatter.5.cloned.1.call-start = ((), (), s32[]{:S(2)}) async-start(), calls=%async_computation.5 | async-start | bytes 17825792 | tf_op jit(solution)/shard_map/reduce_scatter | solution.py:16
Sparse Core Ops, SparseCore 0:
  9.5 77.0 all-gather.2
  131.2 87.0 reduce-scatter.2
  222.0 30.1 all-gather.4
  276.7 177.2 reduce-scatter.4
where the time goes:
time: 463 us
  waiting for transfers between devices  375 us (81%)
  matrix products  64.8 us (14%)
  between operations  13.2 us (3%)
  other arithmetic  9.58 us (2%)
    reduce_scatter x1, waiting for transfers between devices, per_device(): lax.psum_scatter(jnp.dot(hidden, down_weight, preferred_element_type=jnp....  177 us
    reduce_scatter x1, waiting for transfers between devices, per_device(): lax.psum_scatter(partial_both, 'mp', scatter_dimension=0, tiled=True)  87.2 us
    all_gather x1, waiting for transfers between devices, per_device(): piece = lax.all_gather(tokens, 'dp', axis=0, tiled=True)  79.2 us
    all_gather x1, waiting for transfers between devices, per_device(): hidden = lax.all_gather(own_rows, 'mp', axis=0, tiled=True)  30.1 us
    dot_general x1, matrix products, per_device(): jnp.dot(hidden, down_weight, preferred_element_type=jnp.float32)  24.4 us
    dot_general x1, matrix products, per_device(): up_part = jnp.dot(piece, up_weight, preferred_element_type=jnp.float32)  21.3 us
    dot_general x1, matrix products, per_device(): gate_part = jnp.dot(piece, gate_weight, preferred_element_type=jnp.float32)  19.2 us
  transfers between devices with their start and end apart: 4, of which 4 were waited for; matrix products, arithmetic and copies ran while one was open for 0% of the time, Pallas kernels for 0%

commit v1 on v0

--- a/solution.py
+++ b/solution.py
@@ -6,7 +6,14 @@
 
 def per_device(tokens, gate_weight, up_weight, down_weight):
     width = gate_weight.shape[1]
-    piece = lax.all_gather(tokens, "dp", axis=0, tiled=True)
+    count = lax.axis_size("dp")
+    forward = [(i, (i + 1) % count) for i in range(count)]
+    parts = [tokens]
+    for far in range(1, count):
+        parts = [lax.ppermute(parts[0], "dp", forward), *parts]
+    full = jnp.concatenate(parts, axis=0)
+    turn = (lax.axis_index("dp") + 1) * parts[-1].shape[0]
+    piece = jnp.roll(full, turn, axis=0)
     gate_part = jnp.dot(piece, gate_weight, preferred_element_type=jnp.float32)
     up_part = jnp.dot(piece, up_weight, preferred_element_type=jnp.float32)
     partial_both = jnp.concatenate([gate_part, up_part], axis=1)

time: 463 us -> 602 us (1.30)
  waiting for transfers between devices: 375 us -> 465 us
  local copies, waits for them, and re-layouts: 0.01 us -> 46.7 us
    ppermute x0 -> x15, waiting for transfers between devices: none -> 171 us  [per_device(): parts = [lax.ppermute(parts[0], 'dp', forward), *parts]]
    all_gather x1 -> x0, waiting for transfers between devices: 79.2 us -> none  [per_device(): piece = lax.all_gather(tokens, 'dp', axis=0, tiled=True)]
    unnamed x2 -> x65, local copies, waits for them, and re-layouts: 0.01 us -> 45.9 us
  transfers between devices with their start and end apart: 4 -> 18, of which waited for: 4 -> 18; matrix products, arithmetic and copies ran while one was open for 0% -> 0% of each run, Pallas kernels for 0% -> 0%
where the time goes in v1:
time: 602 us; the launch traced here: 601 us
  waiting for transfers between devices  465 us (77%)
  matrix products  66.7 us (11%)
  local copies, waits for them, and re-layouts  46.7 us (8%)
  between operations  13.2 us (2%)
  other arithmetic  9.57 us (2%)
    reduce_scatter x1, waiting for transfers between devices, per_device(): lax.psum_scatter(jnp.dot(hidden, down_weight, preferred_element_type=jnp....  177 us
    ppermute x15, waiting for transfers between devices, per_device(): parts = [lax.ppermute(parts[0], 'dp', forward), *parts]  171 us
    reduce_scatter x1, waiting for transfers between devices, per_device(): lax.psum_scatter(partial_both, 'mp', scatter_dimension=0, tiled=True)  86.1 us
    unnamed x65, local copies, waits for them, and re-layouts  45.9 us
    all_gather x1, waiting for transfers between devices, per_device(): hidden = lax.all_gather(own_rows, 'mp', axis=0, tiled=True)  30.2 us
    dot_general x1, matrix products, per_device(): jnp.dot(hidden, down_weight, preferred_element_type=jnp.float32)  24.4 us
    dot_general x1, matrix products, per_device(): up_part = jnp.dot(piece, up_weight, preferred_element_type=jnp.float32)  21.1 us
    dot_general x1, matrix products, per_device(): gate_part = jnp.dot(piece, gate_weight, preferred_element_type=jnp.float32)  21.1 us
  transfers between devices with their start and end apart: 18, of which 18 were waited for; matrix products, arithmetic and copies ran while one was open for 0% of the time, Pallas kernels for 0%

profile of v1, /device:TPU:0, one launch (start us, length us, event | category | flops | bytes accessed | tf_op | source)
XLA Modules:
  0.0 601.5 jit_solution(12096724149333333235)
XLA Ops:
  7.0 12.1 %collective-permute-done = bf16[32,8192]{1,0:T(8,128)(2,1)S(1)} collective-permute-done((bf16[32,8192]{1,0:T(8,128)(2,1)}, bf16[32,8192]{1,0:T(8,128)(2,1)S(1)}, u32[]{:S(2)}, u32[]{:S(2)}) %collective-permute-start) | collective-permute-done | bytes 524320 | tf_op jit(solution)/shard_map/ppermute | solution.py:13
  19.1 11.3 %collective-permute-done.1 = bf16[32,8192]{1,0:T(8,128)(2,1)S(1)} collective-permute-done((bf16[32,8192]{1,0:T(8,128)(2,1)S(1)}, bf16[32,8192]{1,0:T(8,128)(2,1)S(1)}, u32[]{:S(2)}, u32[]{:S(2)}) %collective-permute-start.1) | collective-permute-done | bytes 524320 | tf_op jit(solution)/shard_map/ppermute | solution.py:13
  30.4 11.3 %collective-permute-done.2 = bf16[32,8192]{1,0:T(8,128)(2,1)S(1)} collective-permute-done((bf16[32,8192]{1,0:T(8,128)(2,1)S(1)}, bf16[32,8192]{1,0:T(8,128)(2,1)S(1)}, u32[]{:S(2)}, u32[]{:S(2)}) %collective-permute-start.2) | collective-permute-done | bytes 524320 | tf_op jit(solution)/shard_map/ppermute | solution.py:13
  41.7 11.3 %collective-permute-done.3 = bf16[32,8192]{1,0:T(8,128)(2,1)S(1)} collective-permute-done((bf16[32,8192]{1,0:T(8,128)(2,1)S(1)}, bf16[32,8192]{1,0:T(8,128)(2,1)S(1)}, u32[]{:S(2)}, u32[]{:S(2)}) %collective-permute-start.3) | collective-permute-done | bytes 524320 | tf_op jit(solution)/shard_map/ppermute | solution.py:13
  53.0 11.3 %collective-permute-done.4 = bf16[32,8192]{1,0:T(8,128)(2,1)S(1)} collective-permute-done((bf16[32,8192]{1,0:T(8,128)(2,1)S(1)}, bf16[32,8192]{1,0:T(8,128)(2,1)S(1)}, u32[]{:S(2)}, u32[]{:S(2)}) %collective-permute-start.4) | collective-permute-done | bytes 524320 | tf_op jit(solution)/shard_map/ppermute | solution.py:13
  64.3 11.3 %collective-permute-done.5 = bf16[32,8192]{1,0:T(8,128)(2,1)S(1)} collective-permute-done((bf16[32,8192]{1,0:T(8,128)(2,1)S(1)}, bf16[32,8192]{1,0:T(8,128)(2,1)S(1)}, u32[]{:S(2)}, u32[]{:S(2)}) %collective-permute-start.5) | collective-permute-done | bytes 524320 | tf_op jit(solution)/shard_map/ppermute | solution.py:13
  76.4 11.3 %collective-permute-done.6 = bf16[32,8192]{1,0:T(8,128)(2,1)S(1)} collective-permute-done((bf16[32,8192]{1,0:T(8,128)(2,1)S(1)}, bf16[32,8192]{1,0:T(8,128)(2,1)S(1)}, u32[]{:S(2)}, u32[]{:S(2)}) %collective-permute-start.6) | collective-permute-done | bytes 524320 | tf_op jit(solution)/shard_map/ppermute | solution.py:13
  88.5 11.3 %collective-permute-done.7 = bf16[32,8192]{1,0:T(8,128)(2,1)S(1)} collective-permute-done((bf16[32,8192]{1,0:T(8,128)(2,1)S(1)}, bf16[32,8192]{1,0:T(8,128)(2,1)S(1)}, u32[]{:S(2)}, u32[]{:S(2)}) %collective-permute-start.7) | collective-permute-done | bytes 524320 | tf_op jit(solution)/shard_map/ppermute | solution.py:13
  100.6 11.3 %collective-permute-done.8 = bf16[32,8192]{1,0:T(8,128)(2,1)S(1)} collective-permute-done((bf16[32,8192]{1,0:T(8,128)(2,1)S(1)}, bf16[32,8192]{1,0:T(8,128)(2,1)S(1)}, u32[]{:S(2)}, u32[]{:S(2)}) %collective-permute-start.8) | collective-permute-done | bytes 524320 | tf_op jit(solution)/shard_map/ppermute | solution.py:13
  112.7 11.3 %collective-permute-done.9 = bf16[32,8192]{1,0:T(8,128)(2,1)S(1)} collective-permute-done((bf16[32,8192]{1,0:T(8,128)(2,1)S(1)}, bf16[32,8192]{1,0:T(8,128)(2,1)S(1)}, u32[]{:S(2)}, u32[]{:S(2)}) %collective-permute-start.9) | collective-permute-done | bytes 524320 | tf_op jit(solution)/shard_map/ppermute | solution.py:13
  124.9 11.3 %collective-permute-done.10 = bf16[32,8192]{1,0:T(8,128)(2,1)S(1)} collective-permute-done((bf16[32,8192]{1,0:T(8,128)(2,1)S(1)}, bf16[32,8192]{1,0:T(8,128)(2,1)S(1)}, u32[]{:S(2)}, u32[]{:S(2)}) %collective-permute-start.10) | collective-permute-done | bytes 524320 | tf_op jit(solution)/shard_map/ppermute | solution.py:13
  137.0 11.3 %collective-permute-done.11 = bf16[32,8192]{1,0:T(8,128)(2,1)S(1)} collective-permute-done((bf16[32,8192]{1,0:T(8,128)(2,1)S(1)}, bf16[32,8192]{1,0:T(8,128)(2,1)S(1)}, u32[]{:S(2)}, u32[]{:S(2)}) %collective-permute-start.11) | collective-permute-done | bytes 524320 | tf_op jit(solution)/shard_map/ppermute | solution.py:13
  149.0 11.3 %collective-permute-done.12 = bf16[32,8192]{1,0:T(8,128)(2,1)S(1)} collective-permute-done((bf16[32,8192]{1,0:T(8,128)(2,1)S(1)}, bf16[32,8192]{1,0:T(8,128)(2,1)S(1)}, u32[]{:S(2)}, u32[]{:S(2)}) %collective-permute-start.12) | collective-permute-done | bytes 524320 | tf_op jit(solution)/shard_map/ppermute | solution.py:13
  161.1 11.4 %collective-permute-done.13 = bf16[32,8192]{1,0:T(8,128)(2,1)} collective-permute-done((bf16[32,8192]{1,0:T(8,128)(2,1)S(1)}, bf16[32,8192]{1,0:T(8,128)(2,1)}, u32[]{:S(2)}, u32[]{:S(2)}) %collective-permute-start.13) | collective-permute-done | bytes 524320 | tf_op jit(solution)/shard_map/ppermute | solution.py:13
  172.6 11.6 %collective-permute-done.14 = bf16[32,8192]{1,0:T(8,128)(2,1)} collective-permute-done((bf16[32,8192]{1,0:T(8,128)(2,1)}, bf16[32,8192]{1,0:T(8,128)(2,1)}, u32[]{:S(2)}, u32[]{:S(2)}) %collective-permute-start.14) | collective-permute-done | bytes 524320 | tf_op jit(solution)/shard_map/ppermute | solution.py:13
  186.0 1.9 constant_dynamic-update-slice_fusion.30
  189.8 1.9 constant_dynamic-update-slice_fusion.28
  191.6 1.9 constant_dynamic-update-slice_fusion.27
  197.3 1.9 constant_dynamic-update-slice_fusion.24
  199.1 1.9 constant_dynamic-update-slice_fusion.23
  201.0 1.9 constant_dynamic-update-slice_fusion.22
  207.1 1.9 constant_dynamic-update-slice_fusion.16
  209.0 1.9 constant_dynamic-update-slice_fusion.15
  224.5 21.1 %fusion.2 = f32[512,1792]{1,0:T(8,128)S(1)} fusion(bf16[8192,1792]{1,0:T(8,128)(2,1)} %param.5, bf16[1024,8192]{1,0:T(8,128)(2,1)} %constant_dynamic-update-slice_fusion, s32[]{:T(128)S(6)} %select_n.14), kind=kOutput, calls=%fused_computation.2 | convolution fusion | flops 15032385536 | bytes 41418756 | tf_op jit(solution)/shard_map/dot_general | solution.py:17
  245.6 21.1 %fusion = f32[512,1792]{1,0:T(8,128)S(1)} fusion(bf16[8192,1792]{1,0:T(8,128)(2,1)} %param.6, bf16[1024,8192]{1,0:T(8,128)(2,1)} %constant_dynamic-update-slice_fusion, s32[]{:T(128)S(6)} %select_n.14), kind=kOutput, calls=%fused_computation | convolution fusion | flops 15032385536 | bytes 41418756 | tf_op jit(solution)/shard_map/dot_general | solution.py:18
  266.8 4.0 pad_maximum_fusion
  271.0 86.1 %reduce-scatter.3.cloned.1.call-done = f32[256,3584]{1,0:T(8,128)} async-done(((f32[512,3584]{1,0:T(8,128)}), f32[256,3584]{1,0:T(8,128)}) %reduce-scatter.3.cloned.1.call-update) | async-done | bytes 3670032 | tf_op jit(solution)/shard_map/reduce_scatter | solution.py:20
  357.1 3.5 fusion.4
  360.7 30.2 %all-gather.2.cloned.1.call-done = bf16[512,1792]{1,0:T(8,128)(2,1)} async-done(((bf16[256,1792]{1,0:T(8,128)(2,1)}), bf16[512,1792]{1,0:T(8,128)(2,1)}) %all-gather.2.cloned.1.call-update) | async-done | bytes 1835024 | tf_op jit(solution)/shard_map/all_gather | solution.py:22
  390.9 24.4 %fusion.7 = f32[512,8192]{1,0:T(8,128)} fusion(bf16[512,1792]{1,0:T(8,128)(2,1)} %all-gather.2.cloned.1.call-done, bf16[1792,8192]{1,0:T(8,128)(2,1)} %param.7), kind=kOutput, calls=%fused_computation.41 | convolution fusion | flops 15032385536 | bytes 47972352 | tf_op jit(solution)/shard_map/dot_general | solution.py:24
  415.4 177.5 %reduce-scatter.5.cloned.1.call-done = f32[32,8192]{1,0:T(8,128)} async-done(((f32[512,8192]{1,0:T(8,128)}), f32[32,8192]{1,0:T(8,128)}) %reduce-scatter.5.cloned.1.call-update) | async-done | bytes 1048592 | tf_op jit(solution)/shard_map/reduce_scatter | solution.py:23
  592.9 2.1 convert_element_type.7
  (79 shorter events, 32.4 us)
Async XLA Ops:
  6.5 217.1 %copy-start = (bf16[32,8192]{1,0:T(8,128)(2,1)S(1)}, bf16[32,8192]{1,0:T(8,128)(2,1)}, u32[]{:S(2)}) copy-start(bf16[32,8192]{1,0:T(8,128)(2,1)} %param.4) | copy-start | bytes 1572868
  6.5 350.6 %reduce-scatter.3.cloned.1.call-start = ((), (), s32[]{:S(2)}) async-start(), calls=%async_computation.2 | async-start | bytes 11010048 | tf_op jit(solution)/shard_map/reduce_scatter | solution.py:20
  6.5 12.6 %collective-permute-start = (bf16[32,8192]{1,0:T(8,128)(2,1)}, bf16[32,8192]{1,0:T(8,128)(2,1)S(1)}, u32[]{:S(2)}, u32[]{:S(2)}) collective-permute-start(bf16[32,8192]{1,0:T(8,128)(2,1)} %param.4), channel_id=1, source_target_pairs={{0,2},{2,4},{4,6},{6,8},{8,10},{10,12},{12,14},{14,16},{16,18},{18... | collective-permute-start | bytes 1572872 | tf_op jit(solution)/shard_map/ppermute | solution.py:13
  19.1 11.3 %collective-permute-start.1 = (bf16[32,8192]{1,0:T(8,128)(2,1)S(1)}, bf16[32,8192]{1,0:T(8,128)(2,1)S(1)}, u32[]{:S(2)}, u32[]{:S(2)}) collective-permute-start(bf16[32,8192]{1,0:T(8,128)(2,1)S(1)} %collective-permute-done), channel_id=1, source_target_pairs={{0,2},{2,4},{4,6},{6,8},{8,10},{10,12},{12,14},{14,16},{16,18},{18... | collective-permute-start | bytes 1572872 | tf_op jit(solution)/shard_map/ppermute | solution.py:13
  30.4 11.3 %collective-permute-start.2 = (bf16[32,8192]{1,0:T(8,128)(2,1)S(1)}, bf16[32,8192]{1,0:T(8,128)(2,1)S(1)}, u32[]{:S(2)}, u32[]{:S(2)}) collective-permute-start(bf16[32,8192]{1,0:T(8,128)(2,1)S(1)} %collective-permute-done.1), channel_id=1, source_target_pairs={{0,2},{2,4},{4,6},{6,8},{8,10},{10,12},{12,14},{14,16},{16,18},{18... | collective-permute-start | bytes 1572872 | tf_op jit(solution)/shard_map/ppermute | solution.py:13
  41.7 11.3 %collective-permute-start.3 = (bf16[32,8192]{1,0:T(8,128)(2,1)S(1)}, bf16[32,8192]{1,0:T(8,128)(2,1)S(1)}, u32[]{:S(2)}, u32[]{:S(2)}) collective-permute-start(bf16[32,8192]{1,0:T(8,128)(2,1)S(1)} %collective-permute-done.2), channel_id=1, source_target_pairs={{0,2},{2,4},{4,6},{6,8},{8,10},{10,12},{12,14},{14,16},{16,18},{18... | collective-permute-start | bytes 1572872 | tf_op jit(solution)/shard_map/ppermute | solution.py:13
  53.0 11.3 %collective-permute-start.4 = (bf16[32,8192]{1,0:T(8,128)(2,1)S(1)}, bf16[32,8192]{1,0:T(8,128)(2,1)S(1)}, u32[]{:S(2)}, u32[]{:S(2)}) collective-permute-start(bf16[32,8192]{1,0:T(8,128)(2,1)S(1)} %collective-permute-done.3), channel_id=1, source_target_pairs={{0,2},{2,4},{4,6},{6,8},{8,10},{10,12},{12,14},{14,16},{16,18},{18... | collective-permute-start | bytes 1572872 | tf_op jit(solution)/shard_map/ppermute | solution.py:13
  64.3 11.3 %collective-permute-start.5 = (bf16[32,8192]{1,0:T(8,128)(2,1)S(1)}, bf16[32,8192]{1,0:T(8,128)(2,1)S(1)}, u32[]{:S(2)}, u32[]{:S(2)}) collective-permute-start(bf16[32,8192]{1,0:T(8,128)(2,1)S(1)} %collective-permute-done.4), channel_id=1, source_target_pairs={{0,2},{2,4},{4,6},{6,8},{8,10},{10,12},{12,14},{14,16},{16,18},{18... | collective-permute-start | bytes 1572872 | tf_op jit(solution)/shard_map/ppermute | solution.py:13
  76.4 11.3 %collective-permute-start.6 = (bf16[32,8192]{1,0:T(8,128)(2,1)S(1)}, bf16[32,8192]{1,0:T(8,128)(2,1)S(1)}, u32[]{:S(2)}, u32[]{:S(2)}) collective-permute-start(bf16[32,8192]{1,0:T(8,128)(2,1)S(1)} %collective-permute-done.5), channel_id=1, source_target_pairs={{0,2},{2,4},{4,6},{6,8},{8,10},{10,12},{12,14},{14,16},{16,18},{18... | collective-permute-start | bytes 1572872 | tf_op jit(solution)/shard_map/ppermute | solution.py:13
  87.7 0.8 copy-start.3
  88.5 11.3 %collective-permute-start.7 = (bf16[32,8192]{1,0:T(8,128)(2,1)S(1)}, bf16[32,8192]{1,0:T(8,128)(2,1)S(1)}, u32[]{:S(2)}, u32[]{:S(2)}) collective-permute-start(bf16[32,8192]{1,0:T(8,128)(2,1)S(1)} %collective-permute-done.6), channel_id=1, source_target_pairs={{0,2},{2,4},{4,6},{6,8},{8,10},{10,12},{12,14},{14,16},{16,18},{18... | collective-permute-start | bytes 1572872 | tf_op jit(solution)/shard_map/ppermute | solution.py:13
  100.6 11.3 %collective-permute-start.8 = (bf16[32,8192]{1,0:T(8,128)(2,1)S(1)}, bf16[32,8192]{1,0:T(8,128)(2,1)S(1)}, u32[]{:S(2)}, u32[]{:S(2)}) collective-permute-start(bf16[32,8192]{1,0:T(8,128)(2,1)S(1)} %collective-permute-done.7), channel_id=1, source_target_pairs={{0,2},{2,4},{4,6},{6,8},{8,10},{10,12},{12,14},{14,16},{16,18},{18... | collective-permute-start | bytes 1572872 | tf_op jit(solution)/shard_map/ppermute | solution.py:13
  111.9 0.8 copy-start.7
  112.7 11.3 %collective-permute-start.9 = (bf16[32,8192]{1,0:T(8,128)(2,1)S(1)}, bf16[32,8192]{1,0:T(8,128)(2,1)S(1)}, u32[]{:S(2)}, u32[]{:S(2)}) collective-permute-start(bf16[32,8192]{1,0:T(8,128)(2,1)S(1)} %collective-permute-done.8), channel_id=1, source_target_pairs={{0,2},{2,4},{4,6},{6,8},{8,10},{10,12},{12,14},{14,16},{16,18},{18... | collective-permute-start | bytes 1572872 | tf_op jit(solution)/shard_map/ppermute | solution.py:13
  124.0 0.8 copy-start.9
  124.9 11.3 %collective-permute-start.10 = (bf16[32,8192]{1,0:T(8,128)(2,1)S(1)}, bf16[32,8192]{1,0:T(8,128)(2,1)S(1)}, u32[]{:S(2)}, u32[]{:S(2)}) collective-permute-start(bf16[32,8192]{1,0:T(8,128)(2,1)S(1)} %collective-permute-done.9), channel_id=1, source_target_pairs={{0,2},{2,4},{4,6},{6,8},{8,10},{10,12},{12,14},{14,16},{16,18},{18... | collective-permute-start | bytes 1572872 | tf_op jit(solution)/shard_map/ppermute | solution.py:13
  137.0 11.3 %collective-permute-start.11 = (bf16[32,8192]{1,0:T(8,128)(2,1)S(1)}, bf16[32,8192]{1,0:T(8,128)(2,1)S(1)}, u32[]{:S(2)}, u32[]{:S(2)}) collective-permute-start(bf16[32,8192]{1,0:T(8,128)(2,1)S(1)} %collective-permute-done.10), channel_id=1, source_target_pairs={{0,2},{2,4},{4,6},{6,8},{8,10},{10,12},{12,14},{14,16},{16,18},{18... | collective-permute-start | bytes 1572872 | tf_op jit(solution)/shard_map/ppermute | solution.py:13
  148.3 0.8 copy-start.13
  149.0 11.3 %collective-permute-start.12 = (bf16[32,8192]{1,0:T(8,128)(2,1)S(1)}, bf16[32,8192]{1,0:T(8,128)(2,1)S(1)}, u32[]{:S(2)}, u32[]{:S(2)}) collective-permute-start(bf16[32,8192]{1,0:T(8,128)(2,1)S(1)} %collective-permute-done.11), channel_id=1, source_target_pairs={{0,2},{2,4},{4,6},{6,8},{8,10},{10,12},{12,14},{14,16},{16,18},{18... | collective-permute-start | bytes 1572872 | tf_op jit(solution)/shard_map/ppermute | solution.py:13
  160.3 0.8 copy-start.15
  161.1 11.4 %collective-permute-start.13 = (bf16[32,8192]{1,0:T(8,128)(2,1)S(1)}, bf16[32,8192]{1,0:T(8,128)(2,1)}, u32[]{:S(2)}, u32[]{:S(2)}) collective-permute-start(bf16[32,8192]{1,0:T(8,128)(2,1)S(1)} %collective-permute-done.12), channel_id=1, source_target_pairs={{0,2},{2,4},{4,6},{6,8},{8,10},{10,12},{12,14},{14,16},{16,18},{18... | collective-permute-start | bytes 1572872 | tf_op jit(solution)/shard_map/ppermute | solution.py:13
  172.6 11.6 %collective-permute-start.14 = (bf16[32,8192]{1,0:T(8,128)(2,1)}, bf16[32,8192]{1,0:T(8,128)(2,1)}, u32[]{:S(2)}, u32[]{:S(2)}) collective-permute-start(bf16[32,8192]{1,0:T(8,128)(2,1)} %collective-permute-done.13), channel_id=1, source_target_pairs={{0,2},{2,4},{4,6},{6,8},{8,10},{10,12},{12,14},{14,16},{16,18},{18... | collective-permute-start | bytes 1572872 | tf_op jit(solution)/shard_map/ppermute | solution.py:13
  172.6 40.2 %copy-start.16 = (bf16[32,8192]{1,0:T(8,128)(2,1)S(1)}, bf16[32,8192]{1,0:T(8,128)(2,1)}, u32[]{:S(2)}) copy-start(bf16[32,8192]{1,0:T(8,128)(2,1)} %copy-done.15) | copy-start | bytes 1572868
  172.6 41.0 %copy-start.14 = (bf16[32,8192]{1,0:T(8,128)(2,1)S(1)}, bf16[32,8192]{1,0:T(8,128)(2,1)}, u32[]{:S(2)}) copy-start(bf16[32,8192]{1,0:T(8,128)(2,1)} %copy-done.13) | copy-start | bytes 1572868
  172.6 41.9 %copy-start.12 = (bf16[32,8192]{1,0:T(8,128)(2,1)S(1)}, bf16[32,8192]{1,0:T(8,128)(2,1)}, u32[]{:S(2)}) copy-start(bf16[32,8192]{1,0:T(8,128)(2,1)} %copy-done.11) | copy-start | bytes 1572868
  172.6 42.7 %copy-start.10 = (bf16[32,8192]{1,0:T(8,128)(2,1)S(1)}, bf16[32,8192]{1,0:T(8,128)(2,1)}, u32[]{:S(2)}) copy-start(bf16[32,8192]{1,0:T(8,128)(2,1)} %copy-done.9) | copy-start | bytes 1572868
  172.6 43.5 %copy-start.8 = (bf16[32,8192]{1,0:T(8,128)(2,1)S(1)}, bf16[32,8192]{1,0:T(8,128)(2,1)}, u32[]{:S(2)}) copy-start(bf16[32,8192]{1,0:T(8,128)(2,1)} %copy-done.7) | copy-start | bytes 1572868
  172.6 44.4 %copy-start.6 = (bf16[32,8192]{1,0:T(8,128)(2,1)S(1)}, bf16[32,8192]{1,0:T(8,128)(2,1)}, u32[]{:S(2)}) copy-start(bf16[32,8192]{1,0:T(8,128)(2,1)} %copy-done.5) | copy-start | bytes 1572868
  172.6 45.2 %copy-start.4 = (bf16[32,8192]{1,0:T(8,128)(2,1)S(1)}, bf16[32,8192]{1,0:T(8,128)(2,1)}, u32[]{:S(2)}) copy-start(bf16[32,8192]{1,0:T(8,128)(2,1)} %copy-done.3) | copy-start | bytes 1572868
  172.6 46.1 %copy-start.2 = (bf16[32,8192]{1,0:T(8,128)(2,1)S(1)}, bf16[32,8192]{1,0:T(8,128)(2,1)}, u32[]{:S(2)}) copy-start(bf16[32,8192]{1,0:T(8,128)(2,1)} %copy-done.1) | copy-start | bytes 1572868
  270.8 120.2 %all-gather.2.cloned.1.call-start = ((), (), s32[]{:S(2)}) async-start(), calls=%async_computation.3 | async-start | bytes 2752512 | tf_op jit(solution)/shard_map/all_gather | solution.py:22
  360.6 232.2 %reduce-scatter.5.cloned.1.call-start = ((), (), s32[]{:S(2)}) async-start(), calls=%async_computation.4 | async-start | bytes 17825792 | tf_op jit(solution)/shard_map/reduce_scatter | solution.py:23
  (3 other events, 2.4 us)
Sparse Core Ops, SparseCore 0:
  270.9 86.1 reduce-scatter.2
  360.8 30.1 all-gather.1
  415.5 177.2 reduce-scatter.4
